TPU v7x, 256 devices: a whole 4x4x8 slice. The times are simulated.
256 devices in a mesh: dp: 4 (over x), ep: 64 (over y, z, core).
Axes of the slice: x: 4, y: 4, z: 8, core: 2. Of those that a mesh axis runs over, the one named last changes fastest.
Arguments:
- tokens: bfloat16 [32768, 2048], P(('dp', 'ep'))
- cotangent: bfloat16 [32768, 2048], P(('dp', 'ep'))
- expert_ids: int32 [32768, 8], P(('dp', 'ep')), may hold values from 0 to 63, all different within a row; in each aligned block of 128 rows (0 to 127, 128 to 255, ...) at most 18 rows name the same one
- route_weights: bfloat16 [32768, 8], P(('dp', 'ep')), may hold values from 0.029907227 to 0.3984375
- weights: bfloat16 [64, 3, 2048, 384], P('ep')
- first_moment: bfloat16 [64, 3, 2048, 384], P('ep', None, 'dp'), may hold values from -4 to 4
- second_moment: bfloat16 [64, 3, 2048, 384], P('ep', None, 'dp'), may hold values from 0.049804688 to 0.5
Outputs:
- token_grad: bfloat16 [32768, 2048], P(('dp', 'ep'))
- routing_grad: bfloat16 [32768, 8], P(('dp', 'ep'))
- new_first: bfloat16 [64, 3, 2048, 384], P('ep', None, 'dp')
- new_second: bfloat16 [64, 3, 2048, 384], P('ep', None, 'dp')
- update: bfloat16 [64, 3, 2048, 384], P('ep', None, 'dp')
Inputs may be any that keep to these rules, and one draw needn't show every extreme that they name: `expert_ids`: among the 128 rows of one device no expert is named by more than 18 rows.
All inputs are finite; a program needn't handle non-finite values.
Results may differ from a plain program's by a relative error of at most 0.0057.
Values may be sent and summed in bfloat16 or wider, within the bound.
No kernel may reach another device: no remote copies, remote signals or barrier semaphores. Data moves between devices by JAX's collectives and lax.ppermute only.
A program may use at most 128 MiB of HBM per device.

v0:
```python
import jax
import jax.numpy as jnp
from jax import lax
from jax.sharding import PartitionSpec as P

ADAM_STEP = 10


def on_device(tokens, cotangent, expert_ids, route_weights, weights, first_moment, second_moment):
    tok_count, model_width = tokens.shape
    topk_count = expert_ids.shape[1]
    local_experts = weights.shape[0]
    hidden_units = weights.shape[3]
    groups = lax.axis_size("ep")
    experts = local_experts * groups
    capacity = (tok_count * topk_count * 9 + 8 * experts - 1) // (8 * experts)
    pairs = tok_count * topk_count
    ids_flat = expert_ids.reshape(-1)
    onehot = (ids_flat[:, None] == jnp.arange(experts, dtype=jnp.int32)[None, :]).astype(jnp.int32)
    position = jnp.sum(jnp.cumsum(onehot, 0) * onehot, 1) - 1
    target = ids_flat * capacity + position
    token_row = jnp.arange(pairs, dtype=jnp.int32) // topk_count
    send_tokens = (
        jnp.zeros((experts * capacity, model_width), jnp.bfloat16).at[target].set(tokens[token_row])
    )
    send_cot = (
        jnp.zeros((experts * capacity, model_width), jnp.bfloat16)
        .at[target]
        .set(cotangent[token_row])
    )
    send_weight = (
        jnp.zeros((experts * capacity,), jnp.bfloat16).at[target].set(route_weights.reshape(-1))
    )
    send_tokens = send_tokens.reshape(experts, capacity, model_width)
    send_cot = send_cot.reshape(experts, capacity, model_width)
    send_weight = send_weight.reshape(experts, capacity)
    recv_x, recv_cot, recv_weight = (
        lax.all_to_all(send_tokens, "ep", split_axis=0, concat_axis=1, tiled=True),
        lax.all_to_all(send_cot, "ep", split_axis=0, concat_axis=1, tiled=True),
        lax.all_to_all(send_weight, "ep", split_axis=0, concat_axis=1, tiled=True),
    )
    w_gate = weights[:, 0]
    w_up = weights[:, 1]
    w_down = weights[:, 2]
    gate_val = jnp.einsum("erd,edh->erh", recv_x, w_gate, preferred_element_type=jnp.float32)
    up_val = jnp.einsum("erd,edh->erh", recv_x, w_up, preferred_element_type=jnp.float32)
    sigmoid_gate = jax.nn.sigmoid(gate_val)
    activated = gate_val * sigmoid_gate
    hidden = lax.optimization_barrier((activated * up_val).astype(jnp.bfloat16))
    back_val = jnp.einsum("erd,edh->erh", recv_cot, w_down, preferred_element_type=jnp.float32)
    route_part = lax.optimization_barrier(
        jnp.sum(hidden.astype(jnp.float32) * back_val, 2).astype(jnp.bfloat16)
    )
    row_weight = recv_weight.astype(jnp.float32)[:, :, None]
    scaled = row_weight * back_val
    dgate = (scaled * up_val * sigmoid_gate * (1.0 + gate_val * (1.0 - sigmoid_gate))).astype(
        jnp.bfloat16
    )
    dup = (scaled * activated).astype(jnp.bfloat16)
    down_cot = (row_weight * recv_cot.astype(jnp.float32)).astype(jnp.bfloat16)
    slot_back = jnp.einsum("erh,edh->erd", dgate, w_gate, preferred_element_type=jnp.float32)
    slot_back = slot_back + jnp.einsum(
        "erh,edh->erd", dup, w_up, preferred_element_type=jnp.float32
    )
    slot_back = lax.optimization_barrier(slot_back.astype(jnp.bfloat16))
    ret_rows, ret_route = (
        lax.all_to_all(slot_back, "ep", split_axis=1, concat_axis=0, tiled=True),
        lax.all_to_all(route_part, "ep", split_axis=1, concat_axis=0, tiled=True),
    )
    picked = ret_rows.reshape(experts * capacity, model_width)[target]
    token_grad = jnp.sum(
        picked.reshape(tok_count, topk_count, model_width).astype(jnp.float32), 1
    ).astype(jnp.bfloat16)
    routing_grad = ret_route.reshape(-1)[target].reshape(tok_count, topk_count)
    grad_local = jnp.stack(
        [
            jnp.einsum("erd,erh->edh", recv_x, dgate, preferred_element_type=jnp.float32),
            jnp.einsum("erd,erh->edh", recv_x, dup, preferred_element_type=jnp.float32),
            jnp.einsum("erd,erh->edh", down_cot, hidden, preferred_element_type=jnp.float32),
        ],
        1,
    )
    grad_share = lax.psum_scatter(grad_local, "dp", scatter_dimension=2, tiled=True)
    square_sum = lax.psum(jnp.sum(grad_share * grad_share), ("dp", "ep"))
    param_count = 3.0 * experts * model_width * hidden_units
    root_mean = jnp.sqrt(square_sum / param_count + 1e-06)
    clip_factor = jnp.minimum(1.0, 0.5 / root_mean)
    clipped = clip_factor * grad_share
    first_next = 0.9 * first_moment.astype(jnp.float32) + 0.1 * clipped
    second_next = 0.95 * second_moment.astype(jnp.float32) + 0.05 * clipped * clipped
    update = (
        first_next
        / (1.0 - 0.9**ADAM_STEP)
        / (jnp.sqrt(second_next / (1.0 - 0.95**ADAM_STEP)) + 1e-08)
    )
    return (
        token_grad,
        routing_grad,
        first_next.astype(jnp.bfloat16),
        second_next.astype(jnp.bfloat16),
        update.astype(jnp.bfloat16),
    )


def solution(mesh):
    in_specs = (
        P(("dp", "ep"), None),
        P(("dp", "ep"), None),
        P(("dp", "ep"), None),
        P(("dp", "ep"), None),
        P("ep", None, None, None),
        P("ep", None, "dp", None),
        P("ep", None, "dp", None),
    )
    out_specs = (
        P(("dp", "ep"), None),
        P(("dp", "ep"), None),
        P("ep", None, "dp", None),
        P("ep", None, "dp", None),
        P("ep", None, "dp", None),
    )
    return jax.shard_map(
        on_device, mesh=mesh, in_specs=in_specs, out_specs=out_specs, check_vma=False
    )
```

profile of v0, /device:TPU:1, one launch (start us, length us, event | category | flops | bytes accessed | tf_op | source)
XLA Modules:
  0.0 766.0 jit_solution(13671669555069183298)
XLA Ops:
  7.2 0.0 copy-start
  7.2 0.7 broadcast_multiply_fusion
  7.9 0.8 copy.45
  8.7 0.1 eq.29
  8.8 0.1 eq.25
  8.9 0.8 copy.49
  9.7 0.1 reshape.350
  9.8 0.1 copy.44
  9.9 0.1 mul.121
  10.0 18.0 %reduce-window.6 = s32[64,8,128]{2,1,0:T(8,128)S(1)} reduce-window(s32[64,8,128]{2,1,0:T(8,128)S(1)} %fusion.38, s32[]{:T(128)} %constant.18.clone.1), window={size=1x1x128 pad=0_0x0_0x127_0}, to_apply=%region_0.0 | reduce-window | flops 8323072 | bytes 524292 | tf_op jit(solution)/shard_map/reduce-window
  28.0 0.1 slice.28
  28.2 0.1 copy.47
  28.4 0.1 copy.48
  28.5 0.1 broadcast_add_fusion
  28.6 0.1 fusion.37
  28.7 7.6 scatter_custom_fusion
  36.3 0.8 all_to_all.23
  37.1 13.4 %all-to-all-start = ((bf16[64,1,18]{2,1,0:T(2,128)(2,1)}), bf16[64,1,18]{2,1,0:T(2,128)(2,1)S(1)}, u32[]{:S(2)}, u32[]{:S(2)}) async-start(bf16[64,1,18]{2,1,0:T(2,128)(2,1)} %all_to_all.23), calls=%async_computation | async-start | bytes 65536 | tf_op jit(solution)/shard_map/all_to_all | solution.py:40
  50.5 23.3 %scatter_custom_fusion.2 = bf16[1152,2048]{1,0:T(8,128)(2,1)} fusion(s32[1024]{0:T(1024)S(1)} %bitcast.83, bf16[128,2048]{1,0:T(8,128)(2,1)S(1)} %copy-done, s32[1024]{0:T(1024)S(1)} %broadcast_clamp_fusion.1, bf16[]{:T(256)} %constant.21.clone.1), kind=kCustom, calls=%fused_computation.17 | custom fusion | bytes 4718594 | tf_op jit(solution)/shard_map/scatter | solution.py:24
  73.8 7.6 reshape.303
  81.4 10.5 %all-to-all-start.2 = ((bf16[64,18,2048]{2,1,0:T(8,128)(2,1)}), bf16[64,18,2048]{2,1,0:T(8,128)(2,1)}, u32[]{:S(2)}, u32[]{:S(2)}) async-start(bf16[64,18,2048]{2,1,0:T(8,128)(2,1)} %reshape.303), calls=%async_computation.2 | async-start | bytes 12582912 | tf_op jit(solution)/shard_map/all_to_all | solution.py:38
  91.9 23.4 %scatter_custom_fusion.1 = bf16[1152,2048]{1,0:T(8,128)(2,1)} fusion(s32[1024]{0:T(1024)S(1)} %bitcast.84, bf16[128,2048]{1,0:T(8,128)(2,1)} %param.8, s32[1024]{0:T(1024)S(1)} %broadcast_clamp_fusion.1, bf16[]{:T(256)} %constant.21.clone.1), kind=kCustom, calls=%fused_computation.19 | custom fusion | bytes 4719104 | tf_op jit(solution)/shard_map/scatter | solution.py:29
  115.3 7.6 reshape.300
  122.9 109.8 %all-to-all-done.2 = bf16[64,18,2048]{2,1,0:T(8,128)(2,1)} async-done(((bf16[64,18,2048]{2,1,0:T(8,128)(2,1)}), bf16[64,18,2048]{2,1,0:T(8,128)(2,1)}, u32[]{:S(2)}, u32[]{:S(2)}) %all-to-all-start.2) | async-done | bytes 4718624 | tf_op jit(solution)/shard_map/all_to_all | solution.py:38
  232.7 6.0 all-to-all-start.1
  238.7 0.0 reduce-scatter.2.cloned.1.call-start
  238.7 0.1 convert_reduce_fusion
  238.8 0.1 reshape.312
  239.0 7.7 %reshape.304 = bf16[1152,2048]{1,0:T(8,128)(2,1)} reshape(bf16[64,18,2048]{2,1,0:T(8,128)(2,1)} %all-to-all-done.2) | data formatting | bytes 9437184 | tf_op jit(solution)/shard_map/reshape.22
  246.7 6.3 fusion.20
  253.0 126.5 %all-to-all-done.1 = bf16[64,18,2048]{2,1,0:T(8,128)(2,1)} async-done(((bf16[64,18,2048]{2,1,0:T(8,128)(2,1)}), bf16[64,18,2048]{2,1,0:T(8,128)(2,1)}, u32[]{:S(2)}, u32[]{:S(2)}) %all-to-all-start.1) | async-done | bytes 4718624 | tf_op jit(solution)/shard_map/all_to_all | solution.py:39
  379.5 7.8 %reshape.301 = bf16[1152,2048]{1,0:T(8,128)(2,1)} reshape(bf16[64,18,2048]{2,1,0:T(8,128)(2,1)} %all-to-all-done.1) | data formatting | bytes 9437184 | tf_op jit(solution)/shard_map/reshape.8
  387.3 5.3 fusion.25
  392.6 5.0 multiply_convert_fusion.2
  397.7 4.5 convolution_bitcast_fusion
  402.2 4.5 convolution_bitcast_fusion.1
  406.7 8.6 %reshape.313 = f32[1,1152,1,1,1,1,2048]{6,1,5,4,3,2,0:T(8,128)} reshape(bf16[64,18,2048]{2,1,0:T(8,128)(2,1)} %all-to-all-done.1) | data formatting | bytes 14155776 | tf_op jit(solution)/shard_map/convert_element_type | solution.py:60
  415.3 6.5 fusion.10
  421.8 4.3 pad_maximum_fusion
  426.1 0.0 reduce-scatter.2.cloned.1.call-update
  426.1 1.7 fusion.16
  427.8 0.8 all_to_all.24
  428.6 5.8 all-to-all-start.4
  434.4 0.0 copy-start.7
  434.4 4.4 fusion.18
  438.8 4.1 fusion.1
  442.9 27.6 %copy.67 = bf16[1,1152,2048]{2,0,1:T(2,128)(2,1)} copy(bf16[1,1152,2048]{2,1,0:T(8,128)(2,1)S(1)} %fusion.1) | data formatting | bytes 9437184 | tf_op jit(solution)/shard_map/optimization_barrier | solution.py:65
  470.5 0.5 broadcast.194
  471.0 29.8 %reduce.8 = bf16[1152,2048]{1,0:T(8,128)(2,1)} reduce(bf16[1152,1,2048]{2,1,0:T(2,128)(2,1)} %bitcast.76, bf16[]{:T(256)} %broadcast.194), dimensions={1}, to_apply=%bitcast.71.reduce_sub_computation | reduce | bytes 9437186
  500.8 9.1 %reshape.393 = bf16[64,2,18432]{2,1,0:T(2,128)(2,1)} reshape(bf16[1152,2048]{1,0:T(8,128)(2,1)} %reduce.8) | data formatting | bytes 9437184
  509.9 10.9 %all-to-all-start.3 = ((bf16[64,2,18432]{2,1,0:T(2,128)(2,1)}), bf16[64,2,18432]{2,1,0:T(2,128)(2,1)}, u32[]{:S(2)}, u32[]{:S(2)}) async-start(bf16[64,2,18432]{2,1,0:T(2,128)(2,1)} %reshape.393), calls=%async_computation.3 | async-start | bytes 9437184 | tf_op jit(solution)/shard_map/all_to_all | solution.py:67
  520.8 0.1 reduce.4
  520.9 0.1 reshape.309
  521.0 6.8 gather_fusion.1
  527.8 0.1 reshape.310
  527.9 0.7 copy.58
  528.6 99.1 %all-to-all-done.3 = bf16[64,2,18432]{2,1,0:T(2,128)(2,1)} async-done(((bf16[64,2,18432]{2,1,0:T(2,128)(2,1)}), bf16[64,2,18432]{2,1,0:T(2,128)(2,1)}, u32[]{:S(2)}, u32[]{:S(2)}) %all-to-all-start.3) | async-done | bytes 4718624 | tf_op jit(solution)/shard_map/all_to_all | solution.py:67
  627.7 20.1 %reshape.394 = bf16[1152,1,2048]{2,1,0:T(2,128)(2,1)} reshape(bf16[64,2,18432]{2,1,0:T(2,128)(2,1)} %all-to-all-done.3) | data formatting | bytes 9437184
  647.8 8.8 %copy.66 = bf16[1,1152,2048]{2,1,0:T(8,128)(2,1)} copy(bf16[1,1152,2048]{2,0,1:T(2,128)(2,1)} %bitcast.77) | data formatting | bytes 9437184
  656.7 11.8 %gather_fusion = bf16[1024,2048]{1,0:T(8,128)(2,1)} fusion(bf16[1152,2048]{1,0:T(8,128)(2,1)} %bitcast.75, s32[1024]{0:T(1024)S(1)} %broadcast_clamp_fusion), kind=kCustom, calls=%fused_computation.2 | custom fusion | bytes 8392704 | tf_op jit(solution)/shard_map/gather | solution.py:70
  668.4 3.0 multiply_reduce_fusion
  671.5 5.9 bitcast_reduce_fusion
  677.4 75.7 %psum.7 = f32[]{:T(128)} all-reduce(f32[]{:T(128)} %multiply_reduce_fusion), channel_id=1, replica_groups=mesh['dp'=4,'ep'=64] {'dp','ep'}, use_global_device_ids=true, to_apply=%region_10.11 | all-reduce | flops 1 | bytes 8 | tf_op jit(solution)/shard_map/psum | solution.py:84
  753.8 5.1 divide_convert_fusion
  (34 shorter events, 0.2 us)
Async XLA Ops:
  7.2 43.4 %copy-start = (bf16[128,2048]{1,0:T(8,128)(2,1)S(1)}, bf16[128,2048]{1,0:T(8,128)(2,1)}, u32[]{:S(2)}) copy-start(bf16[128,2048]{1,0:T(8,128)(2,1)} %param.7) | copy-start | bytes 1572868
  37.1 44.3 %all-to-all-start = ((bf16[64,1,18]{2,1,0:T(2,128)(2,1)}), bf16[64,1,18]{2,1,0:T(2,128)(2,1)S(1)}, u32[]{:S(2)}, u32[]{:S(2)}) async-start(bf16[64,1,18]{2,1,0:T(2,128)(2,1)} %all_to_all.23), calls=%async_computation | async-start | bytes 65536 | tf_op jit(solution)/shard_map/all_to_all | solution.py:40
  81.4 151.3 %all-to-all-start.2 = ((bf16[64,18,2048]{2,1,0:T(8,128)(2,1)}), bf16[64,18,2048]{2,1,0:T(8,128)(2,1)}, u32[]{:S(2)}, u32[]{:S(2)}) async-start(bf16[64,18,2048]{2,1,0:T(8,128)(2,1)} %reshape.303), calls=%async_computation.2 | async-start | bytes 12582912 | tf_op jit(solution)/shard_map/all_to_all | solution.py:38
  232.7 146.8 %all-to-all-start.1 = ((bf16[64,18,2048]{2,1,0:T(8,128)(2,1)}), bf16[64,18,2048]{2,1,0:T(8,128)(2,1)}, u32[]{:S(2)}, u32[]{:S(2)}) async-start(bf16[64,18,2048]{2,1,0:T(8,128)(2,1)} %reshape.300), calls=%async_computation.1 | async-start | bytes 12582912 | tf_op jit(solution)/shard_map/all_to_all | solution.py:39
  238.7 429.8 %reduce-scatter.2.cloned.1.call-start = ((), (), s32[]{:S(2)}) async-start(), calls=%async_computation.6 | async-start | bytes 11796480 | tf_op jit(solution)/shard_map/reduce_scatter | solution.py:83
  379.5 13.0 %slice-start = ((s8[4718592]{0:T(1024)(128)(4,1)}), s8[524288]{0:T(1024)(128)(4,1)S(1)}, s32[]{:S(2)}) async-start(s8[4718592]{0:T(1024)(128)(4,1)} %bitcast.78), calls=%async_computation.7 | async-start | bytes 1048576
  387.3 5.3 slice-start.1
  387.3 5.3 copy-start.8
  392.6 5.1 copy-start.5
  397.7 4.5 copy-start.6
  415.3 6.5 copy-start.3
  415.3 6.5 copy-start.4
  428.6 81.3 %all-to-all-start.4 = ((bf16[1,64,18]{2,0,1:T(2,128)(2,1)}), bf16[1,64,18]{2,0,1:T(2,128)(2,1)S(1)}, u32[]{:S(2)}, u32[]{:S(2)}) async-start(bf16[1,64,18]{2,0,1:T(2,128)(2,1)} %all_to_all.24), calls=%async_computation.4 | async-start | bytes 65536 | tf_op jit(solution)/shard_map/all_to_all | solution.py:68
  434.4 4.4 copy-start.7
  509.9 117.8 %all-to-all-start.3 = ((bf16[64,2,18432]{2,1,0:T(2,128)(2,1)}), bf16[64,2,18432]{2,1,0:T(2,128)(2,1)}, u32[]{:S(2)}, u32[]{:S(2)}) async-start(bf16[64,2,18432]{2,1,0:T(2,128)(2,1)} %reshape.393), calls=%async_computation.3 | async-start | bytes 9437184 | tf_op jit(solution)/shard_map/all_to_all | solution.py:67
  668.4 85.4 %copy-start.2 = (f32[1,3,512,384]{3,2,1,0:T(8,128)S(1)}, f32[1,3,512,384]{3,2,1,0:T(8,128)}, u32[]{:S(2)}) copy-start(f32[1,3,512,384]{3,2,1,0:T(8,128)} %reduce-scatter.2.cloned.1.call-done) | copy-start | bytes 7077892
  671.5 87.5 %copy-start.1 = (bf16[128,2048]{1,0:T(8,128)(2,1)S(1)}, bf16[128,2048]{1,0:T(8,128)(2,1)}, u32[]{:S(2)}) copy-start(bf16[128,2048]{1,0:T(8,128)(2,1)} %param.7) | copy-start | bytes 1572868
Sparse Core Ops, SparseCore 0:
  426.2 87.9 reduce-scatter.1
where the time goes:
time: 773 us; the launch traced here: 766 us
  waiting for transfers between devices  335 us (43%)
  local copies, waits for them, and re-layouts  183 us (24%)
  blocking collectives  75.7 us (10%)
  other arithmetic  69.1 us (9%)
  starting transfers between devices  46.6 us (6%)
  matrix products  40.5 us (5%)
  between operations  15.2 us (2%)
    all_to_all x1, waiting for transfers between devices, on_device(): lax.all_to_all(send_cot, 'ep', split_axis=0, concat_axis=1, tiled=True)  127 us
    all_to_all x1, waiting for transfers between devices, on_device(): lax.all_to_all(send_tokens, 'ep', split_axis=0, concat_axis=1, tiled=True)  110 us
    all_to_all x1, waiting for transfers between devices, on_device(): lax.all_to_all(slot_back, 'ep', split_axis=1, concat_axis=0, tiled=True)  99.1 us
    psum x1, blocking collectives, on_device(): square_sum = lax.psum(jnp.sum(grad_share * grad_share), ('dp', 'ep'))  75.7 us
    unnamed x29, local copies, waits for them, and re-layouts  40.8 us
    unnamed x2, other arithmetic  29.8 us
    optimization_barrier x1, local copies, waits for them, and re-layouts, on_device(): slot_back = lax.optimization_barrier(slot_back.astype(jnp.bfloat16))  27.6 us
    scatter x1, local copies, waits for them, and re-layouts, on_device(): send_cot = jnp.zeros((experts * capacity, model_width), jnp.bfloat16).at[...  23.4 us
  transfers between devices with their start and end apart: 6, of which 3 were waited for; matrix products, arithmetic and copies ran while one was open for 26% of the time, Pallas kernels for 0%

commit v1 on v0

v1 whole, which is shorter than its diff:
```python
import jax
import jax.numpy as jnp
from jax import lax
from jax.experimental.layout import Layout, with_layout_constraint
from jax.sharding import Mesh, PartitionSpec as P

ADAM_STEP = 10
CORES = 2
BF16 = jnp.bfloat16
F32 = jnp.float32
INFO = 128


def plane(mesh):
    dp, ep = mesh.devices.shape
    y = 4
    z = ep // (y * CORES)
    return Mesh(mesh.devices.reshape(dp, y, z, CORES), ("x", "y", "z", "c"))


def on_device(tokens, cotangent, expert_ids, route_weights, weights, first_moment, second_moment):
    tok_count, model_width = tokens.shape
    topk_count = expert_ids.shape[1]
    hidden_units = weights.shape[3]
    ny, nz, nc = lax.axis_size("y"), lax.axis_size("z"), lax.axis_size("c")
    experts = ny * nz * nc
    capacity = (tok_count * topk_count * 9 + 8 * experts - 1) // (8 * experts)
    dests = ny * nc
    slots = nz * capacity
    yi, zi, ci = lax.axis_index("y"), lax.axis_index("z"), lax.axis_index("c")
    me = ((yi * nz + zi) * nc + ci).astype(F32)

    info = jnp.concatenate([expert_ids.astype(BF16), route_weights], 1)
    info = jnp.pad(info, ((0, 0), (0, INFO - 2 * topk_count)))
    info = with_layout_constraint(info, Layout((0, 1)))
    rows = with_layout_constraint(jnp.concatenate([tokens, info], 1), Layout((0, 1)))
    all_x = lax.all_gather(rows, "z", axis=0, tiled=True)
    all_cot = lax.all_gather(cotangent, "z", axis=0, tiled=True)

    ids = all_x[:, model_width : model_width + topk_count].astype(F32)
    dest = jnp.arange(dests, dtype=jnp.int32)
    dest_expert = (((dest // nc) * nz + zi) * nc + dest % nc).astype(F32)
    match = jnp.any(ids[:, :, None] == dest_expert[None, None, :], 1)
    tri = jnp.tril(jnp.ones((tok_count, tok_count), BF16))
    count = jnp.einsum(
        "ab,sbd->sad", tri, match.astype(BF16).reshape(nz, tok_count, dests), preferred_element_type=F32
    )
    base = (jnp.arange(nz, dtype=jnp.int32) * capacity - 1).astype(F32)[:, None, None]
    slot = jnp.where(match, (count + base).reshape(nz * tok_count, dests), -1.0)
    slot = lax.optimization_barrier(slot.T)
    picks = (slot[:, None, :] == jnp.arange(slots, dtype=jnp.int32).astype(F32)[None, :, None]).astype(BF16)
    picks = lax.optimization_barrier(picks.reshape(dests * slots, nz * tok_count))

    def exchange(rows):
        width = rows.shape[1]
        out = lax.all_to_all(rows.reshape(dests, slots, width), ("y", "c"), split_axis=0, concat_axis=0, tiled=True)
        return out.reshape(dests * slots, width)

    recv = exchange(jnp.dot(picks, all_x, preferred_element_type=F32).astype(BF16))
    recv_cot = exchange(jnp.dot(picks, all_cot, preferred_element_type=F32).astype(BF16))
    recv_x = recv[:, :model_width]
    recv_ids = recv[:, model_width : model_width + topk_count].astype(F32)
    recv_rw = recv[:, model_width + topk_count : model_width + 2 * topk_count].astype(F32)
    mine = recv_ids == me
    row_weight = jnp.sum(jnp.where(mine, recv_rw, 0.0), 1, keepdims=True)

    w_gate, w_up, w_down = weights[0, 0], weights[0, 1], weights[0, 2]
    gate_val = jnp.dot(recv_x, w_gate, preferred_element_type=F32)
    up_val = jnp.dot(recv_x, w_up, preferred_element_type=F32)
    sigmoid_gate = jax.nn.sigmoid(gate_val)
    activated = gate_val * sigmoid_gate
    hidden = lax.optimization_barrier((activated * up_val).astype(BF16))
    back_val = jnp.dot(recv_cot, w_down, preferred_element_type=F32)
    route_part = jnp.sum(hidden.astype(F32) * back_val, 1, keepdims=True).astype(BF16)
    scaled = row_weight * back_val
    dgate = (scaled * up_val * sigmoid_gate * (1.0 + gate_val * (1.0 - sigmoid_gate))).astype(BF16)
    dup = (scaled * activated).astype(BF16)
    down_cot = (row_weight * recv_cot.astype(F32)).astype(BF16)
    slot_back = jnp.einsum("rh,dh->rd", dgate, w_gate, preferred_element_type=F32)
    slot_back = slot_back + jnp.einsum("rh,dh->rd", dup, w_up, preferred_element_type=F32)
    route_rows = jnp.where(mine, route_part, jnp.zeros((), BF16))
    route_rows = jnp.pad(route_rows, ((0, 0), (0, INFO - topk_count)))
    send_back = jnp.concatenate([slot_back.astype(BF16), route_rows], 1)
    send_back, grad_x, grad_cot = lax.optimization_barrier((send_back, recv_x, down_cot))
    back_rows = exchange(send_back)
    partial = lax.dot_general(picks, back_rows, (((0,), (0,)), ((), ())), preferred_element_type=F32)
    total = lax.psum_scatter(partial.astype(BF16), "z", scatter_dimension=0, tiled=True)
    token_grad = total[:, :model_width]
    routing_grad = total[:, model_width : model_width + topk_count]

    grad_local = jnp.stack(
        [
            jnp.einsum("rd,rh->dh", grad_x, dgate, preferred_element_type=F32).astype(BF16),
            jnp.einsum("rd,rh->dh", grad_x, dup, preferred_element_type=F32).astype(BF16),
            jnp.einsum("rd,rh->dh", grad_cot, hidden, preferred_element_type=F32).astype(BF16),
        ],
        0,
    )
    grad_share = lax.psum_scatter(grad_local, "x", scatter_dimension=1, tiled=True).astype(F32)[None]
    square = jnp.sum(grad_share * grad_share)
    square = jnp.broadcast_to(square, (experts, 1, 128))
    square = lax.all_to_all(square, ("y", "z", "c"), split_axis=0, concat_axis=0, tiled=True)
    square_sum = lax.psum(jnp.sum(square[:, 0, 0]), "x")
    param_count = 3.0 * experts * model_width * hidden_units
    root_mean = jnp.sqrt(square_sum / param_count + 1e-06)
    clip_factor = jnp.minimum(1.0, 0.5 / root_mean)
    clipped = clip_factor * grad_share
    first_next = 0.9 * first_moment.astype(F32) + 0.1 * clipped
    second_next = 0.95 * second_moment.astype(F32) + 0.05 * clipped * clipped
    update = (
        first_next
        / (1.0 - 0.9**ADAM_STEP)
        / (jnp.sqrt(second_next / (1.0 - 0.95**ADAM_STEP)) + 1e-08)
    )
    return (
        token_grad,
        routing_grad,
        first_next.astype(BF16),
        second_next.astype(BF16),
        update.astype(BF16),
    )


def solution(mesh):
    tok = P(("x", "y", "z", "c"), None)
    ep = ("y", "z", "c")
    state = P(ep, None, "x", None)
    return jax.shard_map(
        on_device,
        mesh=plane(mesh),
        in_specs=(tok, tok, tok, tok, P(ep, None, None, None), state, state),
        out_specs=(tok, tok, state, state, state),
        check_vma=False,
    )
```

time: 773 us -> 376 us (0.49)
  local copies, waits for them, and re-layouts: 183 us -> 9.63 us
  waiting for transfers between devices: 335 us -> 165 us
  other arithmetic: 69.1 us -> 24.3 us
  starting transfers between devices: 46.6 us -> 10.9 us
  matrix products: 40.5 us -> 62.5 us
  blocking collectives: 75.7 us -> 88.2 us
    all_to_all x5 -> x2, waiting for transfers between devices: 335 us -> 45.6 us  [exchange(): lax.all_to_all(rows.reshape(dests, slots, width), ('y', 'c'), split_axis=...]
    all_gather x0 -> x2, waiting for transfers between devices: none -> 98.4 us  [the longest x1 60.1 us: on_device(): all_x = lax.all_gather(rows, 'z', axis=0, tiled=True)]
    all_to_all x0 -> x2, blocking collectives: none -> 78.4 us  [the longest x1 62.5 us: exchange(): lax.all_to_all(rows.reshape(dests, slots, width), ('y', 'c'), split_axis=...]
    psum x1, blocking collectives: 75.7 us -> 9.81 us  [on_device(): square_sum = lax.psum(jnp.sum(square[:, 0, 0]), 'x')]
    scatter x3 -> x0, local copies, waits for them, and re-layouts: 54.2 us -> none  [the longest x1 23.4 us: on_device(): send_cot = jnp.zeros((experts * capacity, model_width), jnp.bfloat16).at[...]
    unnamed x29 -> x19, local copies, waits for them, and re-layouts: 40.8 us -> 0.69 us
    all_to_all x5 -> x2, starting transfers between devices: 46.6 us -> 10.8 us  [exchange(): lax.all_to_all(rows.reshape(dests, slots, width), ('y', 'c'), split_axis=...]
    unnamed x2, other arithmetic: 29.8 us -> 0.01 us
  transfers between devices with their start and end apart: 6 -> 6, of which waited for: 3 -> 5; matrix products, arithmetic and copies ran while one was open for 26% -> 15% of each run, Pallas kernels for 0% -> 0%
where the time goes in v1:
time: 376 us
  waiting for transfers between devices  165 us (44%)
  blocking collectives  88.2 us (23%)
  matrix products  62.5 us (17%)
  other arithmetic  24.3 us (6%)
  between operations  14.7 us (4%)
  starting transfers between devices  10.9 us (3%)
  local copies, waits for them, and re-layouts  9.63 us (3%)
    all_to_all x1, blocking collectives, exchange(): lax.all_to_all(rows.reshape(dests, slots, width), ('y', 'c'), split_axis=...  62.5 us
    all_gather x1, waiting for transfers between devices, on_device(): all_x = lax.all_gather(rows, 'z', axis=0, tiled=True)  60.1 us
    all_to_all x2, waiting for transfers between devices, exchange(): lax.all_to_all(rows.reshape(dests, slots, width), ('y', 'c'), split_axis=...  45.6 us
    all_gather x1, waiting for transfers between devices, on_device(): all_cot = lax.all_gather(cotangent, 'z', axis=0, tiled=True)  38.3 us
    reduce_scatter x1, waiting for transfers between devices, on_device(): lax.psum_scatter(partial.astype(BF16), 'z', scatter_dimension=0, tiled=True)  20.6 us
    all_to_all x1, blocking collectives, on_device(): lax.all_to_all(square, ('y', 'z', 'c'), split_axis=0, concat_axis=0, tile...  15.9 us
    all_to_all x2, starting transfers between devices, exchange(): lax.all_to_all(rows.reshape(dests, slots, width), ('y', 'c'), split_axis=...  10.8 us
    psum x1, blocking collectives, on_device(): square_sum = lax.psum(jnp.sum(square[:, 0, 0]), 'x')  9.81 us
  transfers between devices with their start and end apart: 6, of which 5 were waited for; matrix products, arithmetic and copies ran while one was open for 15% of the time, Pallas kernels for 0%

profile of v1, /device:TPU:1, one launch (start us, length us, event | category | flops | bytes accessed | tf_op | source)
XLA Modules:
  0.0 375.6 jit_solution(4099123066367515721)
XLA Ops:
  7.2 0.0 all-gather.3.cloned.1.call-start
  7.2 0.7 convert_element_type.110
  7.9 0.7 pad_maximum_fusion.1
  8.6 0.1 copy.53
  8.7 1.9 fusion.34
  10.6 0.0 all-gather.3.cloned.1.call-update
  10.6 0.0 all-gather.5.cloned.1.call-start
  10.7 0.7 all-gather.5.cloned.1.call-update
  11.4 0.1 eq.47
  11.5 60.1 %all-gather.3.cloned.1.call-done = bf16[1024,2176]{1,0:T(8,128)(2,1)} async-done(((bf16[128,2176]{1,0:T(8,128)(2,1)}), bf16[1024,2176]{1,0:T(8,128)(2,1)}) %all-gather.3.cloned.1.call-update) | async-done | bytes 4456464 | tf_op jit(solution)/shard_map/all_gather | solution.py:37
  71.6 1.0 slice_convert_fusion
  72.6 0.2 copy.54
  72.8 0.1 compare_reduce_fusion
  72.9 0.1 fusion.33
  73.0 0.5 fusion.3
  73.5 9.6 %convolution_convert_fusion = bf16[1152,2176]{1,0:T(8,128)(2,1)} fusion(bf16[1152,1024]{1,0:T(8,128)(2,1)S(1)} %fusion.3, bf16[1024,2176]{1,0:T(8,128)(2,1)} %all-gather.3.cloned.1.call-done), kind=kOutput, calls=%fused_computation | convolution fusion | flops 5136334848 | bytes 11829248 | tf_op jit(solution)/shard_map/dot_general | solution.py:59
  83.1 5.3 %all-to-all-start = ((bf16[8,144,2176]{2,1,0:T(8,128)(2,1)}), bf16[8,144,2176]{2,1,0:T(8,128)(2,1)}, u32[]{:S(2)}, u32[]{:S(2)}) async-start(bf16[8,144,2176]{2,1,0:T(8,128)(2,1)} %bitcast.80), calls=%async_computation | async-start | bytes 10027008 | tf_op jit(solution)/shard_map/all_to_all | solution.py:56
  88.5 38.3 %all-gather.5.cloned.1.call-done = bf16[1024,2048]{1,0:T(8,128)(2,1)} async-done(((bf16[128,2048]{1,0:T(8,128)(2,1)}), bf16[1024,2048]{1,0:T(8,128)(2,1)}) %all-gather.5.cloned.1.call-update) | async-done | bytes 4194320 | tf_op jit(solution)/shard_map/all_gather | solution.py:38
  126.8 8.8 %convolution_convert_fusion.1 = bf16[1152,2048]{1,0:T(8,128)(2,1)} fusion(bf16[1152,1024]{1,0:T(8,128)(2,1)S(1)} %fusion.3, bf16[1024,2048]{1,0:T(8,128)(2,1)} %all-gather.5.cloned.1.call-done), kind=kOutput, calls=%fused_computation.6 | convolution fusion | flops 4834197504 | bytes 11272192 | tf_op jit(solution)/shard_map/dot_general | solution.py:60
  135.6 10.4 %all-to-all-done = bf16[8,144,2176]{2,1,0:T(8,128)(2,1)} async-done(((bf16[8,144,2176]{2,1,0:T(8,128)(2,1)}), bf16[8,144,2176]{2,1,0:T(8,128)(2,1)}, u32[]{:S(2)}, u32[]{:S(2)}) %all-to-all-start) | async-done | bytes 5013536 | tf_op jit(solution)/shard_map/all_to_all | solution.py:56
  146.0 5.4 %all-to-all-start.1 = ((bf16[8,144,2048]{2,1,0:T(8,128)(2,1)}), bf16[8,144,2048]{2,1,0:T(8,128)(2,1)}, u32[]{:S(2)}, u32[]{:S(2)}) async-start(bf16[8,144,2048]{2,1,0:T(8,128)(2,1)} %bitcast.82), calls=%async_computation.1 | async-start | bytes 9437184 | tf_op jit(solution)/shard_map/all_to_all | solution.py:56
  151.5 0.0 reduce-scatter.5.cloned.1.call-start
  151.5 5.3 %slice.43 = bf16[1152,2048]{1,0:T(8,128)(2,1)} slice(bf16[1152,2176]{1,0:T(8,128)(2,1)} %bitcast.7), slice={[0:1152], [0:2048]} | slice | bytes 9437184 | tf_op jit(solution)/shard_map/slice | solution.py:61
  156.8 1.4 select_reduce_fusion
  158.1 6.4 %fusion.19 = f32[1152,384]{0,1:T(8,128)} fusion(bf16[1,3,2048,384]{3,2,1,0:T(8,128)(2,1)} %param.11, bf16[1152,2176]{1,0:T(8,128)(2,1)} %bitcast.7), kind=kOutput, calls=%fused_computation.39 | convolution fusion | flops 1811939328 | bytes 8060928 | tf_op jit(solution)/shard_map/dot_general | solution.py:69
  164.5 6.3 %fusion.16 = f32[1152,384]{0,1:T(8,128)} fusion(bf16[1,3,2048,384]{3,2,1,0:T(8,128)(2,1)} %param.11, bf16[1152,2176]{1,0:T(8,128)(2,1)} %bitcast.7), kind=kOutput, calls=%fused_computation.36 | convolution fusion | flops 1811939328 | bytes 8060928 | tf_op jit(solution)/shard_map/dot_general | solution.py:68
  170.8 35.1 %all-to-all-done.1 = bf16[8,144,2048]{2,1,0:T(8,128)(2,1)} async-done(((bf16[8,144,2048]{2,1,0:T(8,128)(2,1)}), bf16[8,144,2048]{2,1,0:T(8,128)(2,1)}, u32[]{:S(2)}, u32[]{:S(2)}) %all-to-all-start.1) | async-done | bytes 4718624 | tf_op jit(solution)/shard_map/all_to_all | solution.py:56
  205.9 7.9 %multiply_convert_fusion.2 = (bf16[1152,384]{0,1:T(8,128)(2,1)}, bf16[1152,384]{0,1:T(8,128)(2,1)S(1)}, bf16[1152,384]{0,1:T(8,128)(2,1)S(1)}, f32[1152,384]{0,1:T(8,128)S(1)}) fusion(f32[1152]{0:T(1024)S(1)} %select_reduce_fusion, f32[1152,384]{0,1:T(8,128)} %fusion.16, f32[1152,384]{0,1:T(8,128)} %fusion.19, bf16[1152,2048]{1,0:T(8,128)(2,1)} %bitcast.9, ...), kind=kOutput, calls=%fused_computation.30 | convolution fusion | flops 1819017216 | bytes 14258688 | tf_op jit(solution)/shard_map/dot_general | solution.py:73
  213.8 0.2 multiply_reduce_fusion
  214.0 1.2 broadcast_select_fusion
  215.3 0.0 slice-done.2
  215.3 0.0 slice-done.3
  215.3 2.7 fusion.14
  218.0 0.0 slice-start
  218.0 4.5 %fusion.1 = bf16[1152,2048]{1,0:T(8,128)(2,1)S(1)} fusion(f32[1152,2048]{1,0:T(8,128)S(1)} %fusion.14, bf16[1152,384]{0,1:T(8,128)(2,1)} %get-tuple-element.41, bf16[1,3,2048,384]{3,2,1,0:T(8,128)(2,1)S(1)} %bitcast.86), kind=kOutput, calls=%fused_computation.5 | convolution fusion | flops 1816657920 | bytes 16613376 | tf_op jit(solution)/shard_map/rh,dh->rd/dot_general | solution.py:80
  222.5 0.0 slice-start.1
  222.5 2.7 fusion.2
  225.2 3.2 multiply_convert_fusion
  228.4 0.0 slice-done
  228.5 0.0 slice-done.1
  228.5 0.0 copy-done.4
  228.5 2.8 fusion.6
  231.3 0.0 copy-start.3
  231.3 2.8 fusion.5
  234.2 2.8 fusion.7
  237.0 2.5 pad_maximum_fusion
  239.5 0.0 reduce-scatter.5.cloned.1.call-update
  239.5 0.0 reduce-scatter.3.cloned.1.call-start
  239.6 62.5 %all_to_all.20 = bf16[8,144,2176]{2,1,0:T(8,128)(2,1)S(1)} all-to-all(bf16[8,144,2176]{2,1,0:T(8,128)(2,1)} %bitcast.79), channel_id=1, replica_groups=mesh['x'=4,'y'=4,'z'=8,'c'=2] {'y','c'}, dimensions={0} | all-to-all | bytes 10027008 | tf_op jit(solution)/shard_map/all_to_all | solution.py:56
  302.1 7.9 %convolution_convert_fusion.2 = bf16[1024,2176]{1,0:T(8,128)(2,1)} fusion(bf16[1152,1024]{1,0:T(8,128)(2,1)S(1)} %fusion.3, bf16[1152,2176]{1,0:T(8,128)(2,1)S(1)} %bitcast.81), kind=kOutput, calls=%fused_computation.7 | convolution fusion | flops 5136056320 | bytes 11829248 | tf_op jit(solution)/shard_map/dot_general | solution.py:86
  310.0 0.0 reduce-scatter.3.cloned.1.call-update
  310.0 0.0 reduce-scatter.5.cloned.1.call-done
  310.0 2.6 fusion.10
  312.7 0.7 broadcast_in_dim.44
  313.3 15.9 %all_to_all.21 = f32[64,1,128]{2,1,0:T(1,128)S(1)} all-to-all(f32[64,1,128]{2,1,0:T(1,128)S(1)} %broadcast_in_dim.44), channel_id=1, replica_groups=mesh['x'=4,'y'=4,'z'=8,'c'=2] {'y','z','c'}, dimensions={0} | all-to-all | bytes 65536 | tf_op jit(solution)/shard_map/all_to_all | solution.py:102
  329.2 0.7 slice_reduce_fusion
  329.9 9.8 %psum.7 = f32[]{:T(128)} all-reduce(f32[]{:T(128)} %slice_reduce_fusion), channel_id=1, replica_groups=mesh['x'=4,'y'=4,'z'=8,'c'=2] {'x'}, use_global_device_ids=true, to_apply=%region_7.8 | all-reduce | flops 1 | bytes 8 | tf_op jit(solution)/shard_map/psum | solution.py:103
  340.4 0.0 copy-done
  340.4 0.0 copy-done.1
  340.4 4.8 %divide_convert_fusion = (bf16[1,3,512,384]{3,2,1,0:T(8,128)(2,1)}, bf16[1,3,512,384]{3,2,1,0:T(8,128)(2,1)}, bf16[1,3,512,384]{3,2,1,0:T(8,128)(2,1)}) fusion(bf16[3,512,384]{2,1,0:T(8,128)(2,1)} %reduce-scatter.5.cloned.1.call-done, bf16[1,3,512,384]{3,2,1,0:T(8,128)(2,1)S(1)} %copy-done, bf16[1,3,512,384]{3,2,1,0:T(8,128)(2,1)S(1)} %copy-done.1, f32[]{:T(128)S(6)} %min.3), kind=kLoop, calls=%fused_computation.27 | loop fusion | flops 10616832 | bytes 7077892 | tf_op jit(solution)/shard_map/convert_element_type | solution.py:120
  345.3 20.6 %reduce-scatter.3.cloned.1.call-done = bf16[128,2176]{1,0:T(8,128)(2,1)} async-done(((bf16[1024,2176]{1,0:T(8,128)(2,1)}), bf16[128,2176]{1,0:T(8,128)(2,1)}) %reduce-scatter.3.cloned.1.call-update) | async-done | bytes 557072 | tf_op jit(solution)/shard_map/reduce_scatter | solution.py:87
  365.8 0.8 slice.45
  366.6 0.7 copy.61
  367.2 1.9 slice.44
  (14 shorter events, 0.0 us)
Async XLA Ops:
  7.2 64.5 %all-gather.3.cloned.1.call-start = ((), (), s32[]{:S(2)}) async-start(), calls=%async_computation.6 | async-start | bytes 5013504 | tf_op jit(solution)/shard_map/all_gather | solution.py:37
  10.6 116.2 %all-gather.5.cloned.1.call-start = ((), (), s32[]{:S(2)}) async-start(), calls=%async_computation.7 | async-start | bytes 4718592 | tf_op jit(solution)/shard_map/all_gather | solution.py:38
  83.1 62.9 %all-to-all-start = ((bf16[8,144,2176]{2,1,0:T(8,128)(2,1)}), bf16[8,144,2176]{2,1,0:T(8,128)(2,1)}, u32[]{:S(2)}, u32[]{:S(2)}) async-start(bf16[8,144,2176]{2,1,0:T(8,128)(2,1)} %bitcast.80), calls=%async_computation | async-start | bytes 10027008 | tf_op jit(solution)/shard_map/all_to_all | solution.py:56
  146.0 59.9 %all-to-all-start.1 = ((bf16[8,144,2048]{2,1,0:T(8,128)(2,1)}), bf16[8,144,2048]{2,1,0:T(8,128)(2,1)}, u32[]{:S(2)}, u32[]{:S(2)}) async-start(bf16[8,144,2048]{2,1,0:T(8,128)(2,1)} %bitcast.82), calls=%async_computation.1 | async-start | bytes 9437184 | tf_op jit(solution)/shard_map/all_to_all | solution.py:56
  151.5 158.5 %reduce-scatter.5.cloned.1.call-start = ((), (), s32[]{:S(2)}) async-start(), calls=%async_computation.9 | async-start | bytes 5898240 | tf_op jit(solution)/shard_map/reduce_scatter | solution.py:99
  205.9 9.4 %slice-start.2 = ((s8[4718592]{0:T(1024)(128)(4,1)}), s8[4194304]{0:T(1024)(128)(4,1)S(1)}, s32[]{:S(2)}) async-start(s8[4718592]{0:T(1024)(128)(4,1)} %bitcast.85), calls=%async_computation.12 | async-start | bytes 8388608
  205.9 9.4 %slice-start.3 = ((s8[4718592]{0:T(1024)(128)(4,1)}), s8[524288]{0:T(1024)(128)(4,1)S(1)}, s32[]{:S(2)}) async-start(s8[4718592]{0:T(1024)(128)(4,1)} %bitcast.85), calls=%async_computation.13 | async-start | bytes 1048576
  213.8 4.2 %copy-start.2 = (bf16[1152,384]{0,1:T(8,128)(2,1)}, bf16[1152,384]{0,1:T(8,128)(2,1)S(1)}, u32[]{:S(2)}) copy-start(bf16[1152,384]{0,1:T(8,128)(2,1)S(1)} %get-tuple-element.43) | copy-start | bytes 2654212
  218.0 10.5 %slice-start = ((s8[4718592]{0:T(1024)(128)(4,1)}), s8[4194304]{0:T(1024)(128)(4,1)S(1)}, s32[]{:S(2)}) async-start(s8[4718592]{0:T(1024)(128)(4,1)} %bitcast.83), calls=%async_computation.10 | async-start | bytes 8388608
  222.5 6.0 %slice-start.1 = ((s8[4718592]{0:T(1024)(128)(4,1)}), s8[524288]{0:T(1024)(128)(4,1)S(1)}, s32[]{:S(2)}) async-start(s8[4718592]{0:T(1024)(128)(4,1)} %bitcast.83), calls=%async_computation.11 | async-start | bytes 1048576
  225.2 3.3 copy-start.4
  231.3 2.8 copy-start.3
  239.5 126.3 %reduce-scatter.3.cloned.1.call-start = ((), (), s32[]{:S(2)}) async-start(), calls=%async_computation.8 | async-start | bytes 5013504 | tf_op jit(solution)/shard_map/reduce_scatter | solution.py:87
  310.0 30.5 %copy-start = (bf16[1,3,512,384]{3,2,1,0:T(8,128)(2,1)S(1)}, bf16[1,3,512,384]{3,2,1,0:T(8,128)(2,1)}, u32[]{:S(2)}) copy-start(bf16[1,3,512,384]{3,2,1,0:T(8,128)(2,1)} %param.13) | copy-start | bytes 3538948
  310.0 30.5 %copy-start.1 = (bf16[1,3,512,384]{3,2,1,0:T(8,128)(2,1)S(1)}, bf16[1,3,512,384]{3,2,1,0:T(8,128)(2,1)}, u32[]{:S(2)}) copy-start(bf16[1,3,512,384]{3,2,1,0:T(8,128)(2,1)} %param.12) | copy-start | bytes 3538948
Sparse Core Ops, SparseCore 0:
  10.7 60.8 all-gather.2
  73.4 53.3 all-gather.4
  239.6 50.6 reduce-scatter.4
  310.1 55.6 reduce-scatter.2
